TPU v7x, 256 devices: a whole 4x4x8 slice. The times are simulated.
256 devices in a mesh: dp: 64 (over z, y, core), section: 4 (over x).
Axes of the slice: x: 4, y: 4, z: 8, core: 2. Of those that a mesh axis runs over, the one named last changes fastest.
Arguments:
- query_hidden: bfloat16 [32768, 4096], P('dp', 'section'), may hold values from -0.5 to 0.5
- tool_hidden: bfloat16 [32768, 4096], P('dp', 'section'), may hold values from -0.5 to 0.5
- norm_gain: float32 [4096], P('section'), may hold values from 0.5 to 1.5
- positive_tool: int32 [32768], P('dp'), may hold values from 0 to 511
- hard_owner: int32 [32768, 2], P('dp'), may hold values from 0 to 63, as said below
- hard_row: int32 [32768, 2], P('dp'), may hold values from 0 to 511
- hard_valid: int32 [32768, 2], P('dp'), may hold values from 0 to 1
Outputs:
- query_grad: bfloat16 [32768, 4096], P('dp', 'section')
- tool_grad: bfloat16 [32768, 4096], P('dp', 'section')
- gain_grad: float32 [4096], P('section')
Inputs may be any that keep to these rules, and one draw needn't show every extreme that they name: `hard_owner`: each dp index's valid slots name any one owner at most 32 times; two owners, the same for every dp index and drawn from the seed, are named exactly 32 times by the valid slots of every dp index.
All inputs are finite; a program needn't handle non-finite values.
Results may differ from a plain program's by a relative error of at most 0.0067.
Values may be sent and summed in bfloat16 or wider, within the bound.
A program may use at most 128 MiB of HBM per device.

v0:
```python
import jax
import jax.numpy as jnp
from jax import lax
from jax.sharding import PartitionSpec as P

EPSILON = 1e-06
SOFTMAX_TEMP = 0.05


def softmax_grads(shard_scores, negative_scores, positive, valid_mask):
    selected_rows = lax.broadcasted_iota(jnp.int32, shard_scores.shape, 1) == positive[:, None]
    softmax_weights = jnp.exp(shard_scores / SOFTMAX_TEMP)
    shard_probabilities = softmax_weights / jnp.sum(softmax_weights, axis=1, keepdims=True)
    positive_score = jnp.sum(jnp.where(selected_rows, shard_scores, 0.0), axis=1)
    positive_weight = jnp.exp(positive_score / SOFTMAX_TEMP)
    negative_weights = jnp.where(valid_mask > 0, jnp.exp(negative_scores / SOFTMAX_TEMP), 0.0)
    negative_weight_sum = positive_weight + jnp.sum(negative_weights, axis=1)
    shard_gradients = (
        (
            shard_probabilities
            + jnp.where(selected_rows, (positive_weight / negative_weight_sum - 2.0)[:, None], 0.0)
        )
        / SOFTMAX_TEMP
    ).astype(jnp.bfloat16)
    negative_gradients = (negative_weights / (negative_weight_sum[:, None] * SOFTMAX_TEMP)).astype(
        jnp.bfloat16
    )
    return (shard_gradients, negative_gradients)


def body(query_hidden, tool_hidden, norm_gain, positive_tool, hard_owner, hard_row, hard_valid):
    query_count, features = query_hidden.shape
    per_query = hard_owner.shape[1]
    group_size = lax.axis_size("dp")
    capacity = max(2, 2 * query_count * per_query // group_size)
    query_scaled = query_hidden.astype(jnp.float32) * norm_gain
    tool_scaled = tool_hidden.astype(jnp.float32) * norm_gain
    query_squares, tool_squares = lax.psum(
        (jnp.sum(query_scaled * query_scaled, axis=1), jnp.sum(tool_scaled * tool_scaled, axis=1)),
        "section",
    )
    query_norm = jnp.sqrt(query_squares + EPSILON)
    tool_norm = jnp.sqrt(tool_squares + EPSILON)
    query_unit32 = query_scaled / query_norm[:, None]
    tool_unit32 = tool_scaled / tool_norm[:, None]
    query_unit = query_unit32.astype(jnp.bfloat16)
    tool_unit = tool_unit32.astype(jnp.bfloat16)
    owners = hard_owner.reshape(-1)
    wanted_rows = hard_row.reshape(-1)
    usable = hard_valid.reshape(-1) > 0
    owner_table = (
        (owners[:, None] == jnp.arange(group_size, dtype=jnp.int32)[None, :]) & usable[:, None]
    ).astype(jnp.int32)
    earlier = jnp.cumsum(owner_table, axis=0) - owner_table
    slot_place = jnp.sum(earlier * owner_table, axis=1)
    target = jnp.where(usable, owners * capacity + slot_place, group_size * capacity)
    requests = (
        jnp.zeros((group_size * capacity,), jnp.int32)
        .at[target]
        .set(wanted_rows, mode="drop")
        .reshape(group_size, capacity)
    )
    indices = lax.all_to_all(requests, "dp", split_axis=0, concat_axis=0, tiled=True)
    answers = tool_unit[indices]
    back = lax.all_to_all(answers, "dp", split_axis=0, concat_axis=0, tiled=True)
    lookup = jnp.where(usable, target, 0)
    hard_units = back.reshape(group_size * capacity, features)[lookup].reshape(
        query_count, per_query, features
    )
    local_part = lax.dot_general(
        query_unit, tool_unit, (((1,), (1,)), ((), ())), preferred_element_type=jnp.float32
    )
    hard_part = jnp.einsum("qd,qkd->qk", query_unit, hard_units, preferred_element_type=jnp.float32)
    shard_scores, negative_scores = (
        lax.psum(local_part.astype(jnp.bfloat16), "section").astype(jnp.float32),
        lax.psum(hard_part.astype(jnp.bfloat16), "section").astype(jnp.float32),
    )
    shard_gradients, negative_gradients = softmax_grads(
        shard_scores, negative_scores, positive_tool, hard_valid
    )
    query_pull = jnp.dot(shard_gradients, tool_unit, preferred_element_type=jnp.float32)
    query_pull = query_pull + jnp.einsum(
        "qk,qkd->qd", negative_gradients, hard_units, preferred_element_type=jnp.float32
    )
    tool_pull = lax.dot_general(
        shard_gradients, query_unit, (((0,), (0,)), ((), ())), preferred_element_type=jnp.float32
    )
    slot_queries = jnp.repeat(query_unit, per_query, axis=0)
    returned = negative_gradients.reshape(-1)[:, None].astype(jnp.float32) * slot_queries.astype(
        jnp.float32
    )
    outgoing = (
        jnp.zeros((group_size * capacity, features), jnp.float32)
        .at[target]
        .set(returned, mode="drop")
    )
    arrived = lax.all_to_all(
        outgoing.reshape(group_size, capacity, features).astype(jnp.bfloat16),
        "dp",
        split_axis=0,
        concat_axis=0,
        tiled=True,
    ).astype(jnp.float32)
    tool_pull = tool_pull.at[indices.reshape(-1)].add(arrived.reshape(-1, features))
    query_inner, tool_inner = lax.psum(
        (jnp.sum(query_unit32 * query_pull, axis=1), jnp.sum(tool_unit32 * tool_pull, axis=1)),
        "section",
    )
    query_back = (query_pull - query_unit32 * query_inner[:, None]) / query_norm[:, None]
    tool_back = (tool_pull - tool_unit32 * tool_inner[:, None]) / tool_norm[:, None]
    query_grad = (query_back * norm_gain).astype(jnp.bfloat16)
    tool_grad = (tool_back * norm_gain).astype(jnp.bfloat16)
    gain_terms = jnp.sum(query_back * query_hidden.astype(jnp.float32), axis=0) + jnp.sum(
        tool_back * tool_hidden.astype(jnp.float32), axis=0
    )
    gain_grad = lax.psum(gain_terms, "dp")
    return (query_grad, tool_grad, gain_grad)


def solution(mesh):
    return jax.shard_map(
        body,
        mesh=mesh,
        in_specs=(
            P("dp", "section"),
            P("dp", "section"),
            P("section"),
            P("dp"),
            P("dp", None),
            P("dp", None),
            P("dp", None),
        ),
        out_specs=(P("dp", "section"), P("dp", "section"), P("section")),
        check_vma=False,
    )
```

profile of v0, /device:TPU:1, one launch (start us, length us, event | category | flops | bytes accessed | tf_op | source)
XLA Modules:
  0.0 498.0 jit_solution(5765499487373668806)
XLA Ops:
  7.2 0.7 broadcast_compare_fusion
  7.9 0.2 copy.20
  8.1 0.2 gt.35
  8.3 0.2 gt.34
  8.4 0.8 copy.22
  9.3 0.0 copy-start
  9.3 0.0 copy-start.1
  9.3 0.0 copy-start.4
  9.3 0.2 eq.39
  9.5 0.2 eq.35
  9.7 0.2 gt.33
  9.8 0.8 broadcast_multiply_fusion
  10.7 18.0 %reduce-window.6 = s32[64,8,128]{2,1,0:T(8,128)S(1)} reduce-window(s32[64,8,128]{2,1,0:T(8,128)S(1)} %fusion.28, s32[]{:T(128)} %constant.12.clone.1), window={size=1x1x128 pad=0_0x0_0x127_0}, to_apply=%region_7.8 | reduce-window | flops 8323072 | bytes 524292 | tf_op jit(solution)/shard_map/reduce-window
  28.7 0.1 slice.12
  28.8 0.1 copy.26
  29.0 0.1 copy.27
  29.1 0.1 broadcast_add_fusion
  29.2 0.1 copy.21
  29.4 0.2 mul.109
  29.6 0.1 copy.28
  29.7 0.2 reshape.249
  29.9 0.1 fusion.25
  30.0 4.3 scatter_custom_fusion
  34.3 0.7 all_to_all.14
  35.0 13.1 %all-to-all-start = ((s32[64,1,32]{2,1,0:T(1,128)}), s32[64,1,32]{2,1,0:T(1,128)S(1)}, u32[]{:S(2)}, u32[]{:S(2)}) async-start(s32[64,1,32]{2,1,0:T(1,128)} %bitcast.5), calls=%async_computation | async-start | bytes 65536 | tf_op jit(solution)/shard_map/all_to_all | solution.py:63
  48.2 0.6 fusion.10
  48.8 9.0 %all-reduce.1 = (f32[512]{0:T(512)S(1)}, f32[512]{0:T(512)S(1)}) all-reduce(f32[512]{0:T(512)S(1)} %get-tuple-element.8, f32[512]{0:T(512)S(1)} %get-tuple-element.7), channel_id=1, replica_groups=mesh['dp'=64,'section'=4] {'section'}, use_global_device_ids=true, to_apply=%region_3.0 | all-reduce | flops 1024 | bytes 8192 | tf_op jit(solution)/shard_map/psum | solution.py:38
  57.8 1.8 fusion.33
  59.6 0.0 all-to-all-done
  59.6 0.1 reshape.231
  59.7 9.7 %gather_fusion = bf16[2048,1024]{1,0:T(8,128)(2,1)} fusion(bf16[512,1024]{1,0:T(8,128)(2,1)S(1)} %get-tuple-element.23, s32[2048]{0:T(1024)S(1)} %broadcast_clamp_fusion), kind=kCustom, calls=%fused_computation | custom fusion | bytes 8396800 | tf_op jit(solution)/shard_map/gather | solution.py:64
  69.4 12.0 %all-to-all-start.1 = ((bf16[64,32,1024]{2,1,0:T(8,128)(2,1)}), bf16[64,32,1024]{2,1,0:T(8,128)(2,1)}, u32[]{:S(2)}, u32[]{:S(2)}) async-start(bf16[64,32,1024]{2,1,0:T(8,128)(2,1)} %bitcast.46), calls=%async_computation.1 | async-start | bytes 8388608 | tf_op jit(solution)/shard_map/all_to_all | solution.py:65
  81.4 0.2 all-reduce.4.cloned.1.call-start
  81.6 2.8 convolution_convert_fusion
  84.4 0.0 all-reduce.4.cloned.1.call-update
  84.4 4.3 broadcast_in_dim.32
  88.7 6.0 %convert_element_type.86 = f32[1024,1024]{1,0:T(8,128)} reshape(f32[512,2,1024]{2,1,0:T(2,128)} %broadcast_in_dim.32) | data formatting | bytes 8388608 | tf_op jit(solution)/shard_map/convert_element_type | solution.py:89
  94.7 35.9 %all-reduce.4.cloned.1.call-done = bf16[512,512]{1,0:T(8,128)(2,1)} async-done(((bf16[512,512]{1,0:T(8,128)(2,1)}), bf16[512,512]{1,0:T(8,128)(2,1)}) %all-reduce.4.cloned.1.call-update) | async-done | bytes 524304 | tf_op jit(solution)/shard_map/psum | solution.py:75
  130.7 1.5 fusion.18
  132.2 43.9 %all-to-all-done.1 = bf16[64,32,1024]{2,1,0:T(8,128)(2,1)} async-done(((bf16[64,32,1024]{2,1,0:T(8,128)(2,1)}), bf16[64,32,1024]{2,1,0:T(8,128)(2,1)}, u32[]{:S(2)}, u32[]{:S(2)}) %all-to-all-start.1) | async-done | bytes 4194336 | tf_op jit(solution)/shard_map/all_to_all | solution.py:65
  176.1 8.8 %gather_fusion.1 = bf16[1024,1024]{1,0:T(8,128)(2,1)} fusion(bf16[2048,1024]{1,0:T(8,128)(2,1)} %bitcast.8, s32[1024]{0:T(1024)S(1)} %broadcast_clamp_fusion.1), kind=kCustom, calls=%fused_computation.1 | custom fusion | bytes 4198400 | tf_op jit(solution)/shard_map/gather | solution.py:67
  184.9 4.1 reshape.222
  189.0 6.3 %fusion.14 = bf16[512,1,2]{2,1,0:T(2,128)(2,1)S(1)} fusion(bf16[512,2,1024]{2,1,0:T(2,128)(2,1)} %reshape.222, bf16[512,1024,1]{1,0,2:T(8,128)(2,1)} %bitcast.47), kind=kOutput, calls=%fused_computation.30 | convolution fusion | flops 2097152 | bytes 3147776 | tf_op jit(solution)/shard_map/qd,qkd->qk/dot_general | solution.py:73
  195.3 0.1 copy.32
  195.5 6.0 %psum.52 = bf16[512,2]{0,1:T(2,128)(2,1)S(1)} all-reduce(bf16[512,2]{0,1:T(2,128)(2,1)S(1)} %bitcast.54), channel_id=1, replica_groups=mesh['dp'=64,'section'=4] {'section'}, use_global_device_ids=true, to_apply=%region_11.12 | all-reduce | flops 1024 | bytes 4096 | tf_op jit(solution)/shard_map/psum | solution.py:76
  201.5 0.2 copy.30
  201.7 0.2 reshape.226
  201.9 10.1 %scatter_custom_fusion.1 = f32[2048,1024]{1,0:T(8,128)} fusion(s32[1024]{0:T(1024)S(1)} %bitcast.57, f32[1024,1024]{1,0:T(8,128)} %convert_element_type.86, f32[]{:T(128)} %constant.9.clone.1, f32[1024]{0:T(1024)S(1)} %reshape.226), kind=kCustom, calls=%fused_computation.7 | custom fusion | flops 1048576 | bytes 12587012 | tf_op jit(solution)/shard_map/scatter | solution.py:95
  212.0 6.0 %convert_element_type.87 = bf16[2048,1024]{1,0:T(8,128)(2,1)} convert(f32[2048,1024]{1,0:T(8,128)} %scatter_custom_fusion.1) | non-fusion elementwise | flops 2097152 | bytes 12582912 | tf_op jit(solution)/shard_map/convert_element_type | solution.py:98
  218.0 8.8 %all-to-all-start.2 = ((bf16[64,32,1024]{2,1,0:T(8,128)(2,1)}), bf16[64,32,1024]{2,1,0:T(8,128)(2,1)}, u32[]{:S(2)}, u32[]{:S(2)}) async-start(bf16[64,32,1024]{2,1,0:T(8,128)(2,1)} %bitcast.45), calls=%async_computation.2 | async-start | bytes 8388608 | tf_op jit(solution)/shard_map/all_to_all | solution.py:97
  226.8 0.5 broadcast.204
  227.4 0.7 reduce.3
  228.1 0.1 reshape.223
  228.2 0.2 copy.33
  228.4 3.8 fusion.34
  232.2 3.7 fusion.37
  235.9 85.9 %all-to-all-done.2 = bf16[64,32,1024]{2,1,0:T(8,128)(2,1)} async-done(((bf16[64,32,1024]{2,1,0:T(8,128)(2,1)}), bf16[64,32,1024]{2,1,0:T(8,128)(2,1)}, u32[]{:S(2)}, u32[]{:S(2)}) %all-to-all-start.2) | async-done | bytes 4194336 | tf_op jit(solution)/shard_map/all_to_all | solution.py:97
  321.7 21.0 %scatter_custom_fusion.2 = f32[512,1024]{1,0:T(8,128)} fusion(f32[512,1024]{1,0:T(8,128)} %fusion.34, s32[2048]{0:T(1024)S(1)} %bitcast.55, bf16[2048,1024]{1,0:T(8,128)(2,1)} %bitcast.16), kind=kCustom, calls=%fused_computation.5 | custom fusion | flops 4194304 | bytes 6291456 | tf_op jit(solution)/shard_map/scatter-add | solution.py:104
  342.7 5.2 %multiply_reduce_fusion = (f32[512]{0:T(512)S(1)}, f32[512]{0:T(512)S(1)}, f32[512,1024]{1,0:T(8,128)}) fusion(f32[512,1024]{1,0:T(8,128)} %scatter_custom_fusion.2, f32[512]{0:T(512)S(1)} %get-tuple-element.25, f32[1024]{0:T(1024)S(1)} %copy-done.4, bf16[512,1024]{1,0:T(8,128)(2,1)S(1)} %copy-done.1, f32[512]{0:T(512)S(1)} %get-tuple-element.26, ...), kind=kOutput, calls=%fused_computation.25 | convolution fusion | flops 544734208 | bytes 9979904 | tf_op jit(solution)/shard_map/dot_general | solution.py:81
  347.9 7.7 %all-reduce = (f32[512]{0:T(512)S(1)}, f32[512]{0:T(512)S(1)}) all-reduce(f32[512]{0:T(512)S(1)} %get-tuple-element.6, f32[512]{0:T(512)S(1)} %get-tuple-element.5), channel_id=1, replica_groups=mesh['dp'=64,'section'=4] {'section'}, use_global_device_ids=true, to_apply=%region_14.15 | all-reduce | flops 1024 | bytes 8192 | tf_op jit(solution)/shard_map/psum | solution.py:105
  355.6 2.4 fusion.12
  358.0 2.3 fusion.11
  360.4 128.0 %psum.55 = f32[1024]{0:T(1024)} all-reduce(f32[1024]{0:T(1024)S(1)} %add.119), channel_id=1, replica_groups=mesh['dp'=64,'section'=4] {'dp'}, use_global_device_ids=true, to_apply=%region_21.22 | all-reduce | flops 1024 | bytes 8192 | tf_op jit(solution)/shard_map/psum | solution.py:116
  488.3 2.8 multiply_convert_fusion.1
  (26 shorter events, 0.2 us)
Async XLA Ops:
  7.2 22.4 %copy-start.6 = (s32[512,2]{0,1:T(2,128)S(1)}, s32[512,2]{0,1:T(2,128)}, u32[]{:S(2)}) copy-start(s32[512,2]{0,1:T(2,128)} %param.12) | copy-start | bytes 12292
  9.3 38.9 %copy-start = (bf16[512,1024]{1,0:T(8,128)(2,1)S(1)}, bf16[512,1024]{1,0:T(8,128)(2,1)}, u32[]{:S(2)}) copy-start(bf16[512,1024]{1,0:T(8,128)(2,1)} %param.7) | copy-start | bytes 3145732
  9.3 38.9 %copy-start.1 = (bf16[512,1024]{1,0:T(8,128)(2,1)S(1)}, bf16[512,1024]{1,0:T(8,128)(2,1)}, u32[]{:S(2)}) copy-start(bf16[512,1024]{1,0:T(8,128)(2,1)} %param.8) | copy-start | bytes 3145732
  9.3 38.9 %copy-start.4 = (f32[1024]{0:T(1024)S(1)}, f32[1024]{0:T(1024)}, u32[]{:S(2)}) copy-start(f32[1024]{0:T(1024)} %param.9) | copy-start | bytes 12292
  35.0 24.6 %all-to-all-start = ((s32[64,1,32]{2,1,0:T(1,128)}), s32[64,1,32]{2,1,0:T(1,128)S(1)}, u32[]{:S(2)}, u32[]{:S(2)}) async-start(s32[64,1,32]{2,1,0:T(1,128)} %bitcast.5), calls=%async_computation | async-start | bytes 65536 | tf_op jit(solution)/shard_map/all_to_all | solution.py:63
  69.4 106.7 %all-to-all-start.1 = ((bf16[64,32,1024]{2,1,0:T(8,128)(2,1)}), bf16[64,32,1024]{2,1,0:T(8,128)(2,1)}, u32[]{:S(2)}, u32[]{:S(2)}) async-start(bf16[64,32,1024]{2,1,0:T(8,128)(2,1)} %bitcast.46), calls=%async_computation.1 | async-start | bytes 8388608 | tf_op jit(solution)/shard_map/all_to_all | solution.py:65
  81.4 49.3 %all-reduce.4.cloned.1.call-start = ((), (), s32[]{:S(2)}) async-start(), calls=%async_computation.3 | async-start | bytes 1048576 | tf_op jit(solution)/shard_map/psum | solution.py:75
  88.7 42.0 %copy-start.7 = (s32[512]{0:T(512)S(1)}, s32[512]{0:T(512)}, u32[]{:S(2)}) copy-start(s32[512]{0:T(512)} %param.10) | copy-start | bytes 6148
  189.0 12.5 %copy-start.5 = (s32[512,2]{0,1:T(2,128)S(1)}, s32[512,2]{0,1:T(2,128)}, u32[]{:S(2)}) copy-start(s32[512,2]{0,1:T(2,128)} %param.13) | copy-start | bytes 12292
  218.0 103.7 %all-to-all-start.2 = ((bf16[64,32,1024]{2,1,0:T(8,128)(2,1)}), bf16[64,32,1024]{2,1,0:T(8,128)(2,1)}, u32[]{:S(2)}, u32[]{:S(2)}) async-start(bf16[64,32,1024]{2,1,0:T(8,128)(2,1)} %bitcast.45), calls=%async_computation.2 | async-start | bytes 8388608 | tf_op jit(solution)/shard_map/all_to_all | solution.py:97
  228.4 3.8 copy-start.3
  355.6 2.4 copy-start.2
Sparse Core Ops, SparseCore 0:
  85.1 45.5 all-reduce.3
where the time goes:
time: 499 us; the launch traced here: 498 us
  waiting for transfers between devices  166 us (33%)
  blocking collectives  151 us (30%)
  other arithmetic  69.2 us (14%)
  local copies, waits for them, and re-layouts  42.2 us (8%)
  starting transfers between devices  34.2 us (7%)
  matrix products  21.8 us (4%)
  between operations  14.3 us (3%)
    psum x1, blocking collectives, body(): gain_grad = lax.psum(gain_terms, 'dp')  128 us
    all_to_all x1, waiting for transfers between devices, body(): lax.all_to_all(outgoing.reshape(group_size, capacity, features).astype(jn...  85.9 us
    all_to_all x1, waiting for transfers between devices, body(): lax.all_to_all(answers, 'dp', split_axis=0, concat_axis=0, tiled=True)  43.9 us
    psum x1, waiting for transfers between devices, body(): lax.psum(local_part.astype(jnp.bfloat16), 'section').astype(jnp.float32)  35.9 us
    scatter-add x1, other arithmetic, body(): tool_pull.at[indices.reshape(-1)].add(arrived.reshape(-1, features))  21 us
    another operation x3, other arithmetic  18.2 us
    all_to_all x1, starting transfers between devices, body(): lax.all_to_all(requests, 'dp', split_axis=0, concat_axis=0, tiled=True)  13.1 us
    all_to_all x1, starting transfers between devices, body(): lax.all_to_all(answers, 'dp', split_axis=0, concat_axis=0, tiled=True)  12 us
  transfers between devices with their start and end apart: 4, of which 3 were waited for; matrix products, arithmetic and copies ran while one was open for 5% of the time, Pallas kernels for 0%

commit v1 on v0

--- a/solution.py
+++ b/solution.py
@@ -113,7 +113,8 @@
     gain_terms = jnp.sum(query_back * query_hidden.astype(jnp.float32), axis=0) + jnp.sum(
         tool_back * tool_hidden.astype(jnp.float32), axis=0
     )
-    gain_grad = lax.psum(gain_terms, "dp")
+    v_now = lax.all_gather(gain_terms, "dp")
+    gain_grad = jnp.sum(v_now, axis=0)
     return (query_grad, tool_grad, gain_grad)
 
 

time: 499 us -> 419 us (0.84)
  blocking collectives: 151 us -> 70 us
    psum x1 -> x0, blocking collectives: 128 us -> none  [body(): gain_grad = lax.psum(gain_terms, 'dp')]
    all_gather x0 -> x1, blocking collectives: none -> 47.4 us  [body(): v_now = lax.all_gather(gain_terms, 'dp')]
  transfers between devices with their start and end apart: 4 -> 4, of which waited for: 3 -> 3; matrix products, arithmetic and copies ran while one was open for 5% -> 6% of each run, Pallas kernels for 0% -> 0%
where the time goes in v1:
time: 419 us; the launch traced here: 418 us
  waiting for transfers between devices  166 us (40%)
  blocking collectives  70 us (17%)
  other arithmetic  69.8 us (17%)
  local copies, waits for them, and re-layouts  42.2 us (10%)
  starting transfers between devices  34.2 us (8%)
  matrix products  21.8 us (5%)
  between operations  14.3 us (3%)
    all_to_all x1, waiting for transfers between devices, body(): lax.all_to_all(outgoing.reshape(group_size, capacity, features).astype(jn...  85.9 us
    all_gather x1, blocking collectives, body(): v_now = lax.all_gather(gain_terms, 'dp')  47.4 us
    all_to_all x1, waiting for transfers between devices, body(): lax.all_to_all(answers, 'dp', split_axis=0, concat_axis=0, tiled=True)  43.9 us
    psum x1, waiting for transfers between devices, body(): lax.psum(local_part.astype(jnp.bfloat16), 'section').astype(jnp.float32)  35.9 us
    scatter-add x1, other arithmetic, body(): tool_pull.at[indices.reshape(-1)].add(arrived.reshape(-1, features))  21 us
    another operation x3, other arithmetic  18.2 us
    all_to_all x1, starting transfers between devices, body(): lax.all_to_all(requests, 'dp', split_axis=0, concat_axis=0, tiled=True)  13.1 us
    all_to_all x1, starting transfers between devices, body(): lax.all_to_all(answers, 'dp', split_axis=0, concat_axis=0, tiled=True)  12 us
  transfers between devices with their start and end apart: 4, of which 3 were waited for; matrix products, arithmetic and copies ran while one was open for 6% of the time, Pallas kernels for 0%

profile of v1, /device:TPU:1, one launch (start us, length us, event | category | flops | bytes accessed | tf_op | source)
XLA Modules:
  0.0 418.0 jit_solution(11943338515779134029)
XLA Ops:
  7.2 0.7 broadcast_compare_fusion
  7.9 0.2 copy.31
  8.1 0.2 gt.35
  8.3 0.2 gt.34
  8.4 0.8 copy.33
  9.3 0.0 copy-start
  9.3 0.0 copy-start.1
  9.3 0.0 copy-start.4
  9.3 0.2 eq.39
  9.5 0.2 eq.35
  9.7 0.2 gt.33
  9.8 0.8 broadcast_multiply_fusion
  10.7 18.0 %reduce-window.6 = s32[64,8,128]{2,1,0:T(8,128)S(1)} reduce-window(s32[64,8,128]{2,1,0:T(8,128)S(1)} %fusion.28, s32[]{:T(128)} %constant.12.clone.1), window={size=1x1x128 pad=0_0x0_0x127_0}, to_apply=%region_7.8 | reduce-window | flops 8323072 | bytes 524292 | tf_op jit(solution)/shard_map/reduce-window
  28.7 0.1 slice.12
  28.8 0.1 copy.37
  29.0 0.1 copy.38
  29.1 0.1 broadcast_add_fusion
  29.2 0.1 copy.32
  29.4 0.2 mul.109
  29.6 0.1 copy.39
  29.7 0.2 reshape.261
  29.9 0.1 fusion.25
  30.0 4.3 %scatter_custom_fusion = s32[2048]{0:T(1024)S(1)} fusion(s32[1024]{0:T(1024)S(1)} %bitcast.56, s32[1024]{0:T(1024)S(1)} %reshape.261, s32[]{:T(128)} %constant.12.clone.1), kind=kCustom, calls=%fused_computation.61 | custom fusion | bytes 8196 | tf_op jit(solution)/shard_map/scatter | solution.py:60
  34.3 0.7 all_to_all.14
  35.0 13.1 %all-to-all-start = ((s32[64,1,32]{2,1,0:T(1,128)}), s32[64,1,32]{2,1,0:T(1,128)S(1)}, u32[]{:S(2)}, u32[]{:S(2)}) async-start(s32[64,1,32]{2,1,0:T(1,128)} %bitcast.5), calls=%async_computation | async-start | bytes 65536 | tf_op jit(solution)/shard_map/all_to_all | solution.py:63
  48.2 0.6 fusion.10
  48.8 9.0 %all-reduce.1 = (f32[512]{0:T(512)S(1)}, f32[512]{0:T(512)S(1)}) all-reduce(f32[512]{0:T(512)S(1)} %get-tuple-element.8, f32[512]{0:T(512)S(1)} %get-tuple-element.7), channel_id=1, replica_groups=mesh['dp'=64,'section'=4] {'section'}, use_global_device_ids=true, to_apply=%region_3.0 | all-reduce | flops 1024 | bytes 8192 | tf_op jit(solution)/shard_map/psum | solution.py:38
  57.8 1.8 fusion.33
  59.6 0.1 reshape.243
  59.7 9.7 %gather_fusion = bf16[2048,1024]{1,0:T(8,128)(2,1)} fusion(bf16[512,1024]{1,0:T(8,128)(2,1)S(1)} %get-tuple-element.23, s32[2048]{0:T(1024)S(1)} %broadcast_clamp_fusion), kind=kCustom, calls=%fused_computation | custom fusion | bytes 8396800 | tf_op jit(solution)/shard_map/gather | solution.py:64
  69.4 12.0 %all-to-all-start.1 = ((bf16[64,32,1024]{2,1,0:T(8,128)(2,1)}), bf16[64,32,1024]{2,1,0:T(8,128)(2,1)}, u32[]{:S(2)}, u32[]{:S(2)}) async-start(bf16[64,32,1024]{2,1,0:T(8,128)(2,1)} %bitcast.46), calls=%async_computation.1 | async-start | bytes 8388608 | tf_op jit(solution)/shard_map/all_to_all | solution.py:65
  81.4 0.2 all-reduce.4.cloned.1.call-start
  81.6 2.8 convolution_convert_fusion
  84.4 0.0 all-reduce.4.cloned.1.call-update
  84.4 4.3 %broadcast_in_dim.32 = f32[512,2,1024]{2,1,0:T(2,128)} broadcast(bf16[512,1024]{1,0:T(8,128)(2,1)} %get-tuple-element.22), dimensions={0,2} | broadcast | bytes 5242880 | tf_op jit(solution)/shard_map/broadcast_in_dim | solution.py:88
  88.7 6.0 %convert_element_type.86 = f32[1024,1024]{1,0:T(8,128)} reshape(f32[512,2,1024]{2,1,0:T(2,128)} %broadcast_in_dim.32) | data formatting | bytes 8388608 | tf_op jit(solution)/shard_map/convert_element_type | solution.py:89
  94.7 35.9 %all-reduce.4.cloned.1.call-done = bf16[512,512]{1,0:T(8,128)(2,1)} async-done(((bf16[512,512]{1,0:T(8,128)(2,1)}), bf16[512,512]{1,0:T(8,128)(2,1)}) %all-reduce.4.cloned.1.call-update) | async-done | bytes 524304 | tf_op jit(solution)/shard_map/psum | solution.py:75
  130.7 1.5 fusion.18
  132.2 43.9 %all-to-all-done.1 = bf16[64,32,1024]{2,1,0:T(8,128)(2,1)} async-done(((bf16[64,32,1024]{2,1,0:T(8,128)(2,1)}), bf16[64,32,1024]{2,1,0:T(8,128)(2,1)}, u32[]{:S(2)}, u32[]{:S(2)}) %all-to-all-start.1) | async-done | bytes 4194336 | tf_op jit(solution)/shard_map/all_to_all | solution.py:65
  176.1 8.8 %gather_fusion.1 = bf16[1024,1024]{1,0:T(8,128)(2,1)} fusion(bf16[2048,1024]{1,0:T(8,128)(2,1)} %bitcast.8, s32[1024]{0:T(1024)S(1)} %broadcast_clamp_fusion.1), kind=kCustom, calls=%fused_computation.1 | custom fusion | bytes 4198400 | tf_op jit(solution)/shard_map/gather | solution.py:67
  184.9 4.1 reshape.234
  189.0 6.3 %fusion.14 = bf16[512,1,2]{2,1,0:T(2,128)(2,1)S(1)} fusion(bf16[512,2,1024]{2,1,0:T(2,128)(2,1)} %reshape.234, bf16[512,1024,1]{1,0,2:T(8,128)(2,1)} %bitcast.47), kind=kOutput, calls=%fused_computation.30 | convolution fusion | flops 2097152 | bytes 3147776 | tf_op jit(solution)/shard_map/qd,qkd->qk/dot_general | solution.py:73
  195.3 0.1 copy.43
  195.5 6.0 %psum.45 = bf16[512,2]{0,1:T(2,128)(2,1)S(1)} all-reduce(bf16[512,2]{0,1:T(2,128)(2,1)S(1)} %bitcast.54), channel_id=1, replica_groups=mesh['dp'=64,'section'=4] {'section'}, use_global_device_ids=true, to_apply=%region_11.12 | all-reduce | flops 1024 | bytes 4096 | tf_op jit(solution)/shard_map/psum | solution.py:76
  201.5 0.2 copy.41
  201.7 0.2 reshape.238
  201.9 10.1 %scatter_custom_fusion.1 = f32[2048,1024]{1,0:T(8,128)} fusion(s32[1024]{0:T(1024)S(1)} %bitcast.57, f32[1024,1024]{1,0:T(8,128)} %convert_element_type.86, f32[]{:T(128)} %constant.9.clone.1, f32[1024]{0:T(1024)S(1)} %reshape.238), kind=kCustom, calls=%fused_computation.7 | custom fusion | flops 1048576 | bytes 12587012 | tf_op jit(solution)/shard_map/scatter | solution.py:95
  212.0 6.0 %convert_element_type.87 = bf16[2048,1024]{1,0:T(8,128)(2,1)} convert(f32[2048,1024]{1,0:T(8,128)} %scatter_custom_fusion.1) | non-fusion elementwise | flops 2097152 | bytes 12582912 | tf_op jit(solution)/shard_map/convert_element_type | solution.py:98
  218.0 8.8 %all-to-all-start.2 = ((bf16[64,32,1024]{2,1,0:T(8,128)(2,1)}), bf16[64,32,1024]{2,1,0:T(8,128)(2,1)}, u32[]{:S(2)}, u32[]{:S(2)}) async-start(bf16[64,32,1024]{2,1,0:T(8,128)(2,1)} %bitcast.45), calls=%async_computation.2 | async-start | bytes 8388608 | tf_op jit(solution)/shard_map/all_to_all | solution.py:97
  226.8 0.5 broadcast.204
  227.4 0.7 reduce.3
  228.1 0.1 reshape.235
  228.2 0.2 copy.44
  228.4 3.8 fusion.34
  232.2 3.6 fusion.37
  235.9 85.9 %all-to-all-done.2 = bf16[64,32,1024]{2,1,0:T(8,128)(2,1)} async-done(((bf16[64,32,1024]{2,1,0:T(8,128)(2,1)}), bf16[64,32,1024]{2,1,0:T(8,128)(2,1)}, u32[]{:S(2)}, u32[]{:S(2)}) %all-to-all-start.2) | async-done | bytes 4194336 | tf_op jit(solution)/shard_map/all_to_all | solution.py:97
  321.7 21.0 %scatter_custom_fusion.2 = f32[512,1024]{1,0:T(8,128)} fusion(f32[512,1024]{1,0:T(8,128)} %fusion.34, s32[2048]{0:T(1024)S(1)} %bitcast.55, bf16[2048,1024]{1,0:T(8,128)(2,1)} %bitcast.16), kind=kCustom, calls=%fused_computation.5 | custom fusion | flops 4194304 | bytes 6291456 | tf_op jit(solution)/shard_map/scatter-add | solution.py:104
  342.7 5.2 %multiply_reduce_fusion = (f32[512]{0:T(512)S(1)}, f32[512]{0:T(512)S(1)}, f32[512,1024]{1,0:T(8,128)}) fusion(f32[512,1024]{1,0:T(8,128)} %scatter_custom_fusion.2, f32[512]{0:T(512)S(1)} %get-tuple-element.25, f32[1024]{0:T(1024)S(1)} %copy-done.4, bf16[512,1024]{1,0:T(8,128)(2,1)S(1)} %copy-done.1, f32[512]{0:T(512)S(1)} %get-tuple-element.26, ...), kind=kOutput, calls=%fused_computation.25 | convolution fusion | flops 544734208 | bytes 9979904 | tf_op jit(solution)/shard_map/dot_general | solution.py:81
  347.9 7.7 %all-reduce = (f32[512]{0:T(512)S(1)}, f32[512]{0:T(512)S(1)}) all-reduce(f32[512]{0:T(512)S(1)} %get-tuple-element.6, f32[512]{0:T(512)S(1)} %get-tuple-element.5), channel_id=1, replica_groups=mesh['dp'=64,'section'=4] {'section'}, use_global_device_ids=true, to_apply=%region_14.15 | all-reduce | flops 1024 | bytes 8192 | tf_op jit(solution)/shard_map/psum | solution.py:105
  355.6 2.4 fusion.12
  358.0 2.3 fusion.11
  360.3 47.4 %all-gather = f32[65536]{0:T(1024)S(1)} all-gather(f32[1024]{0:T(1024)S(1)} %add.127), channel_id=2, replica_groups=mesh['dp'=64,'section'=4] {'dp'}, dimensions={0}, use_global_device_ids=true | all-gather | bytes 266240 | tf_op jit(solution)/shard_map/all_gather | solution.py:116
  407.8 0.6 reduce_sum.112
  408.4 2.8 multiply_convert_fusion.1
  (28 shorter events, 0.3 us)
Async XLA Ops:
  7.2 22.4 %copy-start.6 = (s32[512,2]{0,1:T(2,128)S(1)}, s32[512,2]{0,1:T(2,128)}, u32[]{:S(2)}) copy-start(s32[512,2]{0,1:T(2,128)} %param.12) | copy-start | bytes 12292
  9.3 38.9 %copy-start = (bf16[512,1024]{1,0:T(8,128)(2,1)S(1)}, bf16[512,1024]{1,0:T(8,128)(2,1)}, u32[]{:S(2)}) copy-start(bf16[512,1024]{1,0:T(8,128)(2,1)} %param.7) | copy-start | bytes 3145732
  9.3 38.9 %copy-start.1 = (bf16[512,1024]{1,0:T(8,128)(2,1)S(1)}, bf16[512,1024]{1,0:T(8,128)(2,1)}, u32[]{:S(2)}) copy-start(bf16[512,1024]{1,0:T(8,128)(2,1)} %param.8) | copy-start | bytes 3145732
  9.3 38.9 %copy-start.4 = (f32[1024]{0:T(1024)S(1)}, f32[1024]{0:T(1024)}, u32[]{:S(2)}) copy-start(f32[1024]{0:T(1024)} %param.9) | copy-start | bytes 12292
  35.0 24.6 %all-to-all-start = ((s32[64,1,32]{2,1,0:T(1,128)}), s32[64,1,32]{2,1,0:T(1,128)S(1)}, u32[]{:S(2)}, u32[]{:S(2)}) async-start(s32[64,1,32]{2,1,0:T(1,128)} %bitcast.5), calls=%async_computation | async-start | bytes 65536 | tf_op jit(solution)/shard_map/all_to_all | solution.py:63
  69.4 106.7 %all-to-all-start.1 = ((bf16[64,32,1024]{2,1,0:T(8,128)(2,1)}), bf16[64,32,1024]{2,1,0:T(8,128)(2,1)}, u32[]{:S(2)}, u32[]{:S(2)}) async-start(bf16[64,32,1024]{2,1,0:T(8,128)(2,1)} %bitcast.46), calls=%async_computation.1 | async-start | bytes 8388608 | tf_op jit(solution)/shard_map/all_to_all | solution.py:65
  81.4 49.3 %all-reduce.4.cloned.1.call-start = ((), (), s32[]{:S(2)}) async-start(), calls=%async_computation.3 | async-start | bytes 1048576 | tf_op jit(solution)/shard_map/psum | solution.py:75
  88.7 42.0 %copy-start.7 = (s32[512]{0:T(512)S(1)}, s32[512]{0:T(512)}, u32[]{:S(2)}) copy-start(s32[512]{0:T(512)} %param.10) | copy-start | bytes 6148
  189.0 12.5 %copy-start.5 = (s32[512,2]{0,1:T(2,128)S(1)}, s32[512,2]{0,1:T(2,128)}, u32[]{:S(2)}) copy-start(s32[512,2]{0,1:T(2,128)} %param.13) | copy-start | bytes 12292
  218.0 103.7 %all-to-all-start.2 = ((bf16[64,32,1024]{2,1,0:T(8,128)(2,1)}), bf16[64,32,1024]{2,1,0:T(8,128)(2,1)}, u32[]{:S(2)}, u32[]{:S(2)}) async-start(bf16[64,32,1024]{2,1,0:T(8,128)(2,1)} %bitcast.45), calls=%async_computation.2 | async-start | bytes 8388608 | tf_op jit(solution)/shard_map/all_to_all | solution.py:97
  228.4 3.8 copy-start.3
  355.6 2.4 copy-start.2
Sparse Core Ops, SparseCore 0:
  85.1 45.5 all-reduce.3
